TPU v7x, 32 devices: a whole 2x2x4 slice. The times are simulated.
32 devices in a mesh: row: 8 (over y, x, core), col: 4 (over z).
Axes of the slice: x: 2, y: 2, z: 4, core: 2. Of those that a mesh axis runs over, the one named last changes fastest.
Arguments:
- final_amp: bfloat16 [8, 32, 128, 440], P('row', 'col'), may hold values from -0.19921875 to 0.19921875
- initial_amp: bfloat16 [4, 32, 128, 440], P('col', 'row'), may hold values from -0.19921875 to 0.19921875
- pair_final: int32 [8, 4, 128], P('row', 'col'), may hold values from 0 to 31
- pair_initial: int32 [8, 4, 128], P('row', 'col'), may hold values from 0 to 31
- map_final: int32 [8, 32, 440], P('row', 'col'), may hold values from 0 to 439, each once within a row
- map_initial: int32 [4, 32, 440], P('col', 'row'), may hold values from 0 to 439, each once within a row
- counts: int32 [8, 4], P('row', 'col'), may hold values from 16 to 128, as said below
Outputs:
- density: float32 [440, 440], replicated
Inputs may be any that keep to these rules, and one draw needn't show every extreme that they name: `counts`: slots at or past a cell's count are ignored. Exactly one cell of every draw has 128 live slots.
All inputs are finite; a program needn't handle non-finite values.
Results may differ from a plain program's by a relative error of at most 0.0003.
Values may be sent and summed in bfloat16 or wider, within the bound.
A program may use at most 64 MiB of HBM per device.

v0:
```python
import jax
import jax.numpy as jnp
from jax import lax
from jax.sharding import PartitionSpec as P

GROUP = 32


def permute_columns(blocks, orbital_map):
    return jnp.take(blocks, orbital_map, axis=1)


def shards(final_amp, initial_amp, pair_final, pair_initial, map_final, map_initial, counts):
    own_final = jax.vmap(permute_columns)(final_amp[0], map_final[0])[None]
    own_initial = jax.vmap(permute_columns)(initial_amp[0], map_initial[0])[None]
    row_seg = lax.all_gather(own_final, "col", axis=1, tiled=True)[0]
    column_seg = lax.all_gather(own_initial, "row", axis=1, tiled=True)[0]
    slots_final = pair_final[0, 0]
    slots_initial = pair_initial[0, 0]
    live_count = counts[0, 0]
    orbitals = final_amp.shape[3]
    group_size = GROUP

    def advance(index, summed):
        first_slot = index * group_size
        which_final = lax.dynamic_slice_in_dim(slots_final, first_slot, group_size)
        which_initial = lax.dynamic_slice_in_dim(slots_initial, first_slot, group_size)
        live_mask = first_slot + jnp.arange(group_size, dtype=jnp.int32) < live_count
        left = jnp.take(row_seg, which_final, axis=0)
        right = jnp.take(column_seg, which_initial, axis=0)
        left = jnp.where(live_mask[:, None, None], left, jnp.zeros_like(left))
        product = lax.dot_general(
            left.reshape(-1, orbitals),
            right.reshape(-1, orbitals),
            (((0,), (0,)), ((), ())),
            preferred_element_type=jnp.float32,
        )
        return summed + product

    turns = (live_count + group_size - 1) // group_size
    partial_density = lax.fori_loop(0, turns, advance, jnp.zeros((orbitals, orbitals), jnp.float32))
    band = lax.psum_scatter(partial_density, "col", scatter_dimension=0, tiled=True)
    band = lax.psum(band, "row")
    density = lax.all_gather(band, "col", axis=0, tiled=True)
    return density


def solution(mesh):
    placed = (
        P("row", "col", None, None),
        P("col", "row", None, None),
        P("row", "col", None),
        P("row", "col", None),
        P("row", "col", None),
        P("col", "row", None),
        P("row", "col"),
    )
    return jax.shard_map(shards, mesh=mesh, in_specs=placed, out_specs=P(), check_vma=False)
```

profile of v0, /device:TPU:0, one launch (start us, length us, event | category | flops | bytes accessed | tf_op | source)
XLA Modules:
  0.0 321.1 jit_solution(12124861493017973160)
XLA Ops:
  6.5 0.8 fusion.18
  7.3 0.7 compare_and_fusion.2
  8.2 30.8 %gather_fusion.2 = bf16[3520,128]{1,0:T(8,128)(2,1)S(1)} fusion(bf16[8,128,440]{1,2,0:T(8,128)(2,1)S(1)} %bitcast.44, s32[3520]{0:T(1024)S(1)} %reshape.110), kind=kCustom, calls=%fused_computation.2 | custom fusion | bytes 1830400 | tf_op jit(solution)/shard_map/vmap(jit(_take))/gather | solution.py:10
  39.0 1.4 broadcast_select_fusion
  40.5 15.7 %gather_fusion.3 = bf16[1760,128]{1,0:T(8,128)(2,1)S(1)} fusion(bf16[4,128,440]{1,2,0:T(8,128)(2,1)S(1)} %bitcast.45, s32[1760]{0:T(1024)S(1)} %reshape.116), kind=kCustom, calls=%fused_computation.3 | custom fusion | bytes 915200 | tf_op jit(solution)/shard_map/vmap(jit(_take))/gather | solution.py:10
  56.3 1.1 broadcast_select_fusion.1
  58.2 56.1 %all-gather.4.cloned.1.call-done = bf16[1,32,128,440]{2,3,0,1:T(8,128)(2,1)} async-done(((bf16[1,8,128,440]{2,3,0,1:T(8,128)(2,1)}), bf16[1,32,128,440]{2,3,0,1:T(8,128)(2,1)}) %all-gather.4.cloned.1.call-update) | async-done | bytes 3604496 | tf_op jit(solution)/shard_map/all_gather | solution.py:16
  114.3 6.4 %copy.18 = bf16[32,128,440]{2,1,0:T(8,128)(2,1)} copy(bf16[32,128,440]{1,2,0:T(8,128)(2,1)} %bitcast.47) | data formatting | bytes 7208960 | tf_op jit(solution)/shard_map/while | solution.py:41
  120.7 28.2 %all-gather.6.cloned.1.call-done = bf16[1,32,128,440]{2,3,0,1:T(8,128)(2,1)} async-done(((bf16[1,4,128,440]{2,3,0,1:T(8,128)(2,1)}), bf16[1,32,128,440]{2,3,0,1:T(8,128)(2,1)}) %all-gather.6.cloned.1.call-update) | async-done | bytes 3604496 | tf_op jit(solution)/shard_map/all_gather | solution.py:17
  148.9 6.5 %copy.19 = bf16[32,128,440]{2,1,0:T(8,128)(2,1)} copy(bf16[32,128,440]{1,2,0:T(8,128)(2,1)} %bitcast.48) | data formatting | bytes 7208960 | tf_op jit(solution)/shard_map/while | solution.py:41
  155.3 0.1 broadcast_in_dim.43
  155.5 33.5 %while.10 = (s32[]{:T(128)}, f32[440,440]{1,0:T(8,128)S(1)}, s32[]{:T(128)}, s32[]{:T(128)}, s32[128]{0:T(128)S(1)}, /*index=5*/bf16[32,128,440]{2,1,0:T(8,128)(...) while((s32[]{:T(128)}, f32[440,440]{1,0:T(8,128)S(1)}, ...), condition=%wide.region_1.3_spmd, body=%wide.region_0.0_spmd.sunk | while | flops 1591574016 | bytes 23185264 | solution.py:41
  155.5 0.1 compare_and_fusion.5
  155.6 5.0 %gather_fusion = bf16[32,128,440]{2,1,0:T(8,128)(2,1)} fusion(bf16[32,128,440]{2,1,0:T(8,128)(2,1)} %get-tuple-element.169, s32[1024]{0:T(1024)S(1)} %pad_clamp_fusion.4), kind=kCustom, calls=%fused_computation.1.clone.clone.1 | custom fusion | bytes 7209088 | tf_op jit(solution)/shard_map/while/body/jit(_take)/gather | solution.py:30
  160.6 4.9 %gather_fusion.1 = bf16[32,128,440]{2,1,0:T(8,128)(2,1)} fusion(bf16[32,128,440]{2,1,0:T(8,128)(2,1)} %get-tuple-element.167, s32[1024]{0:T(1024)S(1)} %pad_clamp_fusion.5), kind=kCustom, calls=%fused_computation.clone.clone.1 | custom fusion | bytes 7209088 | tf_op jit(solution)/shard_map/while/body/jit(_take)/gather | solution.py:29
  165.5 0.7 add_compare_fusion.2
  166.1 6.1 %fusion.25 = f32[440,440]{1,0:T(8,128)S(1)} fusion(f32[440,440]{1,0:T(8,128)S(1)} %get-tuple-element.151, bf16[32,128,440]{2,1,0:T(8,128)(2,1)} %gather_fusion, pred[32]{0:T(512)(128)(4,1)S(1)} %get-tuple-element.135, bf16[32,128,440]{2,1,0:T(8,128)(2,1)} %gather_fusion.1, pred[32]{0:T(512)(128)(4,1)S(1)} %get-tuple-element.137, ...), kind=kOutput, calls=%fused_computation.13.clone.1 | convolution fusion | flops 1591571456 | bytes 8757856 | tf_op jit(solution)/shard_map/while/body/dot_general | solution.py:32
  172.3 5.0 %gather_fusion = bf16[32,128,440]{2,1,0:T(8,128)(2,1)} fusion(bf16[32,128,440]{2,1,0:T(8,128)(2,1)} %get-tuple-element.169, s32[1024]{0:T(1024)S(1)} %pad_clamp_fusion.4), kind=kCustom, calls=%fused_computation.1.clone.clone.1 | custom fusion | bytes 7209088 | tf_op jit(solution)/shard_map/while/body/jit(_take)/gather | solution.py:30
  177.3 4.9 %gather_fusion.1 = bf16[32,128,440]{2,1,0:T(8,128)(2,1)} fusion(bf16[32,128,440]{2,1,0:T(8,128)(2,1)} %get-tuple-element.167, s32[1024]{0:T(1024)S(1)} %pad_clamp_fusion.5), kind=kCustom, calls=%fused_computation.clone.clone.1 | custom fusion | bytes 7209088 | tf_op jit(solution)/shard_map/while/body/jit(_take)/gather | solution.py:29
  182.2 0.7 add_compare_fusion.2
  182.9 6.1 %fusion.25 = f32[440,440]{1,0:T(8,128)S(1)} fusion(f32[440,440]{1,0:T(8,128)S(1)} %get-tuple-element.151, bf16[32,128,440]{2,1,0:T(8,128)(2,1)} %gather_fusion, pred[32]{0:T(512)(128)(4,1)S(1)} %get-tuple-element.135, bf16[32,128,440]{2,1,0:T(8,128)(2,1)} %gather_fusion.1, pred[32]{0:T(512)(128)(4,1)S(1)} %get-tuple-element.137, ...), kind=kOutput, calls=%fused_computation.13.clone.1 | convolution fusion | flops 1591571456 | bytes 8757856 | tf_op jit(solution)/shard_map/while/body/dot_general | solution.py:32
  188.9 22.8 %fusion = f32[112,440]{1,0:T(8,128)S(1)} fusion(f32[440,440]{1,0:T(8,128)S(1)} %get-tuple-element.49), kind=kCustom, calls=%all-reduce-scatter | all-reduce-scatter fusion | flops 197121 | bytes 972032
  211.7 2.1 collective-permute-start
  213.9 0.6 dynamic-slice.4
  215.1 0.2 collective-permute-done
  215.3 0.2 concatenate.6
  215.6 0.7 constant_dynamic-slice_fusion
  216.3 74.9 %all-reduce.4.cloned.1.call-done = f32[110,440]{1,0:T(8,128)} async-done(((f32[110,440]{1,0:T(8,128)}), f32[110,440]{1,0:T(8,128)}) %all-reduce.4.cloned.1.call-update) | async-done | bytes 193616 | tf_op jit(solution)/shard_map/psum | solution.py:43
  291.2 1.1 copy.20
  292.3 20.9 %all-gather = f32[4,110,440]{1,2,0:T(8,128)S(1)} all-gather(f32[1,110,440]{1,2,0:T(8,128)S(1)} %copy.20), channel_id=1, replica_groups=mesh['row'=8,'col'=4] {'col'}, dimensions={0}, use_global_device_ids=true | all-gather | bytes 968000 | tf_op jit(solution)/shard_map/all_gather | solution.py:44
  313.2 0.4 copy.21
  313.6 1.0 reshape.125
  (28 shorter events, 0.5 us)
Async XLA Ops:
  6.5 1.6 copy-start
  6.5 107.7 %all-gather.4.cloned.1.call-start = ((), (), s32[]{:S(2)}) async-start(), calls=%async_computation | async-start | bytes 4505600 | tf_op jit(solution)/shard_map/all_gather | solution.py:16
  8.2 32.3 %copy-start.2 = (s32[1,4,440]{2,1,0:T(4,128)S(1)}, s32[1,4,440]{2,1,0:T(4,128)}, u32[]{:S(2)}) copy-start(s32[1,4,440]{2,1,0:T(4,128)} %param.16) | copy-start | bytes 21124
  8.2 32.4 %copy-start.1 = (bf16[1,4,128,440]{2,3,1,0:T(8,128)(2,1)S(1)}, bf16[1,4,128,440]{2,3,1,0:T(8,128)(2,1)}, u32[]{:S(2)}) copy-start(bf16[1,4,128,440]{2,3,1,0:T(8,128)(2,1)} %param.12) | copy-start | bytes 1351684
  40.4 108.5 %all-gather.6.cloned.1.call-start = ((), (), s32[]{:S(2)}) async-start(), calls=%async_computation.1 | async-start | bytes 4055040 | tf_op jit(solution)/shard_map/all_gather | solution.py:17
  57.4 233.8 %all-reduce.4.cloned.1.call-start = ((), (), s32[]{:S(2)}) async-start(), calls=%async_computation.2 | async-start | bytes 458752 | tf_op jit(solution)/shard_map/psum | solution.py:43
  148.9 6.6 %copy-start.3 = (s32[1,1,128]{2,1,0:T(1,128)S(1)}, s32[1,1,128]{2,1,0:T(1,128)}, u32[]{:S(2)}) copy-start(s32[1,1,128]{2,1,0:T(1,128)} %param.13) | copy-start | bytes 1540
  148.9 6.6 %copy-start.4 = (s32[1,1,128]{2,1,0:T(1,128)S(1)}, s32[1,1,128]{2,1,0:T(1,128)}, u32[]{:S(2)}) copy-start(s32[1,1,128]{2,1,0:T(1,128)} %param.14) | copy-start | bytes 1540
  155.5 58.4 %copy-start.5 = (u32[32]{0:T(128)S(1)}, u32[32]{0:T(128)}, u32[]{:S(2)}) copy-start(u32[32]{0:T(128)} %constant.104) | copy-start | bytes 388
  211.7 3.6 %collective-permute-start = (f32[6,440]{1,0:T(8,128)S(1)}, f32[6,440]{1,0:T(8,128)S(1)}, u32[]{:S(2)}, u32[]{:S(2)}) collective-permute-start(f32[6,440]{1,0:T(8,128)S(1)} %slice.8), channel_id=1, source_target_pairs={{0,1},{1,2},{2,3},{4,5},{5,6},{6,7},{8,9},{9,10},{10,11},{12,13},{... | collective-permute-start | bytes 31688
Sparse Core Ops, SparseCore 0:
  40.5 73.7 all-gather.3
  116.2 32.6 all-gather.5
  216.4 74.7 all-reduce.3
where the time goes:
time: 322 us; the launch traced here: 321 us
  waiting for transfers between devices  159 us (49%)
  local copies, waits for them, and re-layouts  83.4 us (26%)
  blocking collectives  43.7 us (14%)
  between operations  14.6 us (5%)
  matrix products  12.1 us (4%)
  other arithmetic  5.57 us (2%)
    psum x1, waiting for transfers between devices, shards(): band = lax.psum(band, 'row')  74.9 us
    all_gather x1, waiting for transfers between devices, shards(): row_seg = lax.all_gather(own_final, 'col', axis=1, tiled=True)[0]  56.1 us
    gather x4, local copies, waits for them, and re-layouts, permute_columns(): return jnp.take(blocks, orbital_map, axis=1)  46.6 us
    all_gather x1, waiting for transfers between devices, shards(): column_seg = lax.all_gather(own_initial, 'row', axis=1, tiled=True)[0]  28.2 us
    unnamed x1, blocking collectives  22.8 us
    all_gather x1, blocking collectives, shards(): density = lax.all_gather(band, 'col', axis=0, tiled=True)  20.9 us
    while x2, local copies, waits for them, and re-layouts, shards(): lax.fori_loop(0, turns, advance, jnp.zeros((orbitals, orbitals), jnp.floa...  12.9 us
    dot_general x2, matrix products, advance(): lax.dot_general(left.reshape(-1, orbitals), right.reshape(-1, orbitals),...  12.1 us
  transfers between devices with their start and end apart: 4, of which 4 were waited for; matrix products, arithmetic and copies ran while one was open for 7% of the time, Pallas kernels for 0%

commit v1 on v0

--- a/solution.py
+++ b/solution.py
@@ -1,9 +1,31 @@
+import functools
 import jax
 import jax.numpy as jnp
 from jax import lax
 from jax.sharding import PartitionSpec as P
 
 GROUP = 32
+
+
+def use_trails(arr, axis_id):
+    world = lax.psum(1, axis_id)
+    entries = []
+    for ii in range(world):
+        entries.append((ii, (ii + 1) % world))
+
+    def group_roots(before):
+        if len(before) == world:
+            return before
+        near = lax.ppermute(before[0], axis_id, entries)
+        return group_roots([near, *before])
+
+    outcome_arr = group_roots([arr])
+    f_now = jnp.concatenate(outcome_arr, 0)
+    met_up = lax.axis_index(axis_id)
+    return jnp.roll(f_now, (met_up + 1) * arr.shape[0], 0)
+
+
+run_keys = functools.partial(use_trails, axis_id="col")
 
 
 def permute_columns(blocks, orbital_map):
@@ -41,7 +63,7 @@
     partial_density = lax.fori_loop(0, turns, advance, jnp.zeros((orbitals, orbitals), jnp.float32))
     band = lax.psum_scatter(partial_density, "col", scatter_dimension=0, tiled=True)
     band = lax.psum(band, "row")
-    density = lax.all_gather(band, "col", axis=0, tiled=True)
+    density = run_keys(band)
     return density
 
 

time: 322 us -> 330 us (1.025)
  waiting for transfers between devices: 159 us -> 185 us
  blocking collectives: 43.7 us -> 22.8 us
    ppermute x0 -> x3, waiting for transfers between devices: none -> 25.4 us  [group_roots(): near = lax.ppermute(before[0], axis_id, entries)]
    all_gather x1 -> x0, blocking collectives: 20.9 us -> none  [shards(): density = lax.all_gather(band, 'col', axis=0, tiled=True)]
  transfers between devices with their start and end apart: 4 -> 7, of which waited for: 4 -> 7; matrix products, arithmetic and copies ran while one was open for 7% -> 7% of each run, Pallas kernels for 0% -> 0%
where the time goes in v1:
time: 330 us; the launch traced here: 329 us
  waiting for transfers between devices  185 us (56%)
  local copies, waits for them, and re-layouts  85.1 us (26%)
  blocking collectives  22.8 us (7%)
  between operations  14.6 us (4%)
  matrix products  12.1 us (4%)
  other arithmetic  5.57 us (2%)
  starting transfers between devices  3.7 us (1%)
    psum x1, waiting for transfers between devices, shards(): band = lax.psum(band, 'row')  74.9 us
    all_gather x1, waiting for transfers between devices, shards(): row_seg = lax.all_gather(own_final, 'col', axis=1, tiled=True)[0]  56.1 us
    gather x4, local copies, waits for them, and re-layouts, permute_columns(): return jnp.take(blocks, orbital_map, axis=1)  46.6 us
    all_gather x1, waiting for transfers between devices, shards(): column_seg = lax.all_gather(own_initial, 'row', axis=1, tiled=True)[0]  28.2 us
    ppermute x3, waiting for transfers between devices, group_roots(): near = lax.ppermute(before[0], axis_id, entries)  25.4 us
    unnamed x1, blocking collectives  22.8 us
    while x2, local copies, waits for them, and re-layouts, shards(): lax.fori_loop(0, turns, advance, jnp.zeros((orbitals, orbitals), jnp.floa...  12.9 us
    dot_general x2, matrix products, advance(): lax.dot_general(left.reshape(-1, orbitals), right.reshape(-1, orbitals),...  12.1 us
  transfers between devices with their start and end apart: 7, of which 7 were waited for; matrix products, arithmetic and copies ran while one was open for 7% of the time, Pallas kernels for 0%

profile of v1, /device:TPU:0, one launch (start us, length us, event | category | flops | bytes accessed | tf_op | source)
XLA Modules:
  0.0 328.7 jit_solution(8888139109966720143)
XLA Ops:
  6.5 0.8 fusion.18
  7.3 0.7 compare_and_fusion.2
  8.2 30.8 %gather_fusion.2 = bf16[3520,128]{1,0:T(8,128)(2,1)S(1)} fusion(bf16[8,128,440]{1,2,0:T(8,128)(2,1)S(1)} %bitcast.43, s32[3520]{0:T(1024)S(1)} %reshape.110), kind=kCustom, calls=%fused_computation.2 | custom fusion | bytes 1830400 | tf_op jit(solution)/shard_map/vmap(jit(_take))/gather | solution.py:32
  39.0 1.4 broadcast_select_fusion
  40.5 15.7 %gather_fusion.3 = bf16[1760,128]{1,0:T(8,128)(2,1)S(1)} fusion(bf16[4,128,440]{1,2,0:T(8,128)(2,1)S(1)} %bitcast.44, s32[1760]{0:T(1024)S(1)} %reshape.116), kind=kCustom, calls=%fused_computation.3 | custom fusion | bytes 915200 | tf_op jit(solution)/shard_map/vmap(jit(_take))/gather | solution.py:32
  56.3 1.1 broadcast_select_fusion.1
  58.2 56.1 %all-gather.3.cloned.1.call-done = bf16[1,32,128,440]{2,3,0,1:T(8,128)(2,1)} async-done(((bf16[1,8,128,440]{2,3,0,1:T(8,128)(2,1)}), bf16[1,32,128,440]{2,3,0,1:T(8,128)(2,1)}) %all-gather.3.cloned.1.call-update) | async-done | bytes 3604496 | tf_op jit(solution)/shard_map/all_gather | solution.py:38
  114.3 6.4 %copy.14 = bf16[32,128,440]{2,1,0:T(8,128)(2,1)} copy(bf16[32,128,440]{1,2,0:T(8,128)(2,1)} %bitcast.46) | data formatting | bytes 7208960 | tf_op jit(solution)/shard_map/while | solution.py:63
  120.7 28.2 %all-gather.5.cloned.1.call-done = bf16[1,32,128,440]{2,3,0,1:T(8,128)(2,1)} async-done(((bf16[1,4,128,440]{2,3,0,1:T(8,128)(2,1)}), bf16[1,32,128,440]{2,3,0,1:T(8,128)(2,1)}) %all-gather.5.cloned.1.call-update) | async-done | bytes 3604496 | tf_op jit(solution)/shard_map/all_gather | solution.py:39
  148.9 6.5 %copy.15 = bf16[32,128,440]{2,1,0:T(8,128)(2,1)} copy(bf16[32,128,440]{1,2,0:T(8,128)(2,1)} %bitcast.47) | data formatting | bytes 7208960 | tf_op jit(solution)/shard_map/while | solution.py:63
  155.5 33.5 %while.10 = (s32[]{:T(128)}, f32[440,440]{1,0:T(8,128)S(1)}, s32[]{:T(128)}, s32[]{:T(128)}, s32[128]{0:T(128)S(1)}, /*index=5*/bf16[32,128,440]{2,1,0:T(8,128)(...) while((s32[]{:T(128)}, f32[440,440]{1,0:T(8,128)S(1)}, ...), condition=%wide.region_1.3_spmd, body=%wide.region_0.0_spmd.sunk | while | flops 1591574016 | bytes 23185264 | solution.py:63
  155.6 5.0 %gather_fusion = bf16[32,128,440]{2,1,0:T(8,128)(2,1)} fusion(bf16[32,128,440]{2,1,0:T(8,128)(2,1)} %get-tuple-element.169, s32[1024]{0:T(1024)S(1)} %pad_clamp_fusion.4), kind=kCustom, calls=%fused_computation.1.clone.clone.1 | custom fusion | bytes 7209088 | tf_op jit(solution)/shard_map/while/body/jit(_take)/gather | solution.py:52
  160.6 4.9 %gather_fusion.1 = bf16[32,128,440]{2,1,0:T(8,128)(2,1)} fusion(bf16[32,128,440]{2,1,0:T(8,128)(2,1)} %get-tuple-element.167, s32[1024]{0:T(1024)S(1)} %pad_clamp_fusion.5), kind=kCustom, calls=%fused_computation.clone.clone.1 | custom fusion | bytes 7209088 | tf_op jit(solution)/shard_map/while/body/jit(_take)/gather | solution.py:51
  165.5 0.7 add_compare_fusion.2
  166.1 6.0 %fusion.25 = f32[440,440]{1,0:T(8,128)S(1)} fusion(f32[440,440]{1,0:T(8,128)S(1)} %get-tuple-element.151, bf16[32,128,440]{2,1,0:T(8,128)(2,1)} %gather_fusion, pred[32]{0:T(512)(128)(4,1)S(1)} %get-tuple-element.135, bf16[32,128,440]{2,1,0:T(8,128)(2,1)} %gather_fusion.1, pred[32]{0:T(512)(128)(4,1)S(1)} %get-tuple-element.137, ...), kind=kOutput, calls=%fused_computation.13.clone.1 | convolution fusion | flops 1591571456 | bytes 8757856 | tf_op jit(solution)/shard_map/while/body/dot_general | solution.py:54
  172.3 5.0 %gather_fusion = bf16[32,128,440]{2,1,0:T(8,128)(2,1)} fusion(bf16[32,128,440]{2,1,0:T(8,128)(2,1)} %get-tuple-element.169, s32[1024]{0:T(1024)S(1)} %pad_clamp_fusion.4), kind=kCustom, calls=%fused_computation.1.clone.clone.1 | custom fusion | bytes 7209088 | tf_op jit(solution)/shard_map/while/body/jit(_take)/gather | solution.py:52
  177.3 4.9 %gather_fusion.1 = bf16[32,128,440]{2,1,0:T(8,128)(2,1)} fusion(bf16[32,128,440]{2,1,0:T(8,128)(2,1)} %get-tuple-element.167, s32[1024]{0:T(1024)S(1)} %pad_clamp_fusion.5), kind=kCustom, calls=%fused_computation.clone.clone.1 | custom fusion | bytes 7209088 | tf_op jit(solution)/shard_map/while/body/jit(_take)/gather | solution.py:51
  182.2 0.7 add_compare_fusion.2
  182.9 6.1 %fusion.25 = f32[440,440]{1,0:T(8,128)S(1)} fusion(f32[440,440]{1,0:T(8,128)S(1)} %get-tuple-element.151, bf16[32,128,440]{2,1,0:T(8,128)(2,1)} %gather_fusion, pred[32]{0:T(512)(128)(4,1)S(1)} %get-tuple-element.135, bf16[32,128,440]{2,1,0:T(8,128)(2,1)} %gather_fusion.1, pred[32]{0:T(512)(128)(4,1)S(1)} %get-tuple-element.137, ...), kind=kOutput, calls=%fused_computation.13.clone.1 | convolution fusion | flops 1591571456 | bytes 8757856 | tf_op jit(solution)/shard_map/while/body/dot_general | solution.py:54
  188.9 22.8 %fusion = f32[112,440]{1,0:T(8,128)S(1)} fusion(f32[440,440]{1,0:T(8,128)S(1)} %get-tuple-element.49), kind=kCustom, calls=%all-reduce-scatter | all-reduce-scatter fusion | flops 197121 | bytes 972032
  211.7 2.1 collective-permute-start.3
  213.9 0.6 dynamic-slice.4
  215.1 0.2 collective-permute-done.3
  215.3 0.2 concatenate.13
  215.6 0.7 constant_dynamic-slice_fusion
  216.3 74.9 %all-reduce.4.cloned.1.call-done = f32[110,440]{1,0:T(8,128)} async-done(((f32[110,440]{1,0:T(8,128)}), f32[110,440]{1,0:T(8,128)}) %all-reduce.4.cloned.1.call-update) | async-done | bytes 193616 | tf_op jit(solution)/shard_map/psum | solution.py:65
  291.2 1.5 collective-permute-start
  292.7 8.5 %collective-permute-done = f32[110,440]{1,0:T(8,128)S(1)} collective-permute-done((f32[110,440]{1,0:T(8,128)}, f32[110,440]{1,0:T(8,128)S(1)}, u32[]{:S(2)}, u32[]{:S(2)}) %collective-permute-start) | collective-permute-done | bytes 193632 | tf_op jit(solution)/shard_map/ppermute | solution.py:19
  301.2 8.9 %collective-permute-done.1 = f32[110,440]{1,0:T(8,128)S(1)} collective-permute-done((f32[110,440]{1,0:T(8,128)S(1)}, f32[110,440]{1,0:T(8,128)S(1)}, u32[]{:S(2)}, u32[]{:S(2)}) %collective-permute-start.1) | collective-permute-done | bytes 193632 | tf_op jit(solution)/shard_map/ppermute | solution.py:19
  310.1 8.0 %collective-permute-done.2 = f32[110,440]{1,0:T(8,128)S(1)} collective-permute-done((f32[110,440]{1,0:T(8,128)S(1)}, f32[110,440]{1,0:T(8,128)S(1)}, u32[]{:S(2)}, u32[]{:S(2)}) %collective-permute-start.2) | collective-permute-done | bytes 193632 | tf_op jit(solution)/shard_map/ppermute | solution.py:19
  318.1 3.0 concatenate.6
  321.2 1.0 constant_dynamic-slice_fusion.1
  (32 shorter events, 0.6 us)
Async XLA Ops:
  6.5 1.6 copy-start
  6.5 107.7 %all-gather.3.cloned.1.call-start = ((), (), s32[]{:S(2)}) async-start(), calls=%async_computation | async-start | bytes 4505600 | tf_op jit(solution)/shard_map/all_gather | solution.py:38
  8.2 32.3 %copy-start.2 = (s32[1,4,440]{2,1,0:T(4,128)S(1)}, s32[1,4,440]{2,1,0:T(4,128)}, u32[]{:S(2)}) copy-start(s32[1,4,440]{2,1,0:T(4,128)} %param.16) | copy-start | bytes 21124
  8.2 32.4 %copy-start.1 = (bf16[1,4,128,440]{2,3,1,0:T(8,128)(2,1)S(1)}, bf16[1,4,128,440]{2,3,1,0:T(8,128)(2,1)}, u32[]{:S(2)}) copy-start(bf16[1,4,128,440]{2,3,1,0:T(8,128)(2,1)} %param.12) | copy-start | bytes 1351684
  40.4 108.5 %all-gather.5.cloned.1.call-start = ((), (), s32[]{:S(2)}) async-start(), calls=%async_computation.1 | async-start | bytes 4055040 | tf_op jit(solution)/shard_map/all_gather | solution.py:39
  57.4 233.8 %all-reduce.4.cloned.1.call-start = ((), (), s32[]{:S(2)}) async-start(), calls=%async_computation.2 | async-start | bytes 458752 | tf_op jit(solution)/shard_map/psum | solution.py:65
  148.9 6.6 %copy-start.3 = (s32[1,1,128]{2,1,0:T(1,128)S(1)}, s32[1,1,128]{2,1,0:T(1,128)}, u32[]{:S(2)}) copy-start(s32[1,1,128]{2,1,0:T(1,128)} %param.13) | copy-start | bytes 1540
  148.9 6.6 %copy-start.4 = (s32[1,1,128]{2,1,0:T(1,128)S(1)}, s32[1,1,128]{2,1,0:T(1,128)}, u32[]{:S(2)}) copy-start(s32[1,1,128]{2,1,0:T(1,128)} %param.14) | copy-start | bytes 1540
  155.5 58.4 %copy-start.5 = (u32[32]{0:T(128)S(1)}, u32[32]{0:T(128)}, u32[]{:S(2)}) copy-start(u32[32]{0:T(128)} %constant.127) | copy-start | bytes 388
  211.7 3.6 %collective-permute-start.3 = (f32[6,440]{1,0:T(8,128)S(1)}, f32[6,440]{1,0:T(8,128)S(1)}, u32[]{:S(2)}, u32[]{:S(2)}) collective-permute-start(f32[6,440]{1,0:T(8,128)S(1)} %slice.8), channel_id=1, source_target_pairs={{0,1},{1,2},{2,3},{4,5},{5,6},{6,7},{8,9},{9,10},{10,11},{12,13},{... | collective-permute-start | bytes 31688
  291.2 10.0 %collective-permute-start = (f32[110,440]{1,0:T(8,128)}, f32[110,440]{1,0:T(8,128)S(1)}, u32[]{:S(2)}, u32[]{:S(2)}) collective-permute-start(f32[110,440]{1,0:T(8,128)} %all-reduce.4.cloned.1.call-done), channel_id=1, source_target_pairs={{0,1},{1,2},{2,3},{3,0},{4,5},{5,6},{6,7},{7,4},{8,9},{9,10},{10,1... | collective-permute-start | bytes 580808 | tf_op jit(solution)/shard_map/ppermute | solution.py:19
  301.2 8.9 %collective-permute-start.1 = (f32[110,440]{1,0:T(8,128)S(1)}, f32[110,440]{1,0:T(8,128)S(1)}, u32[]{:S(2)}, u32[]{:S(2)}) collective-permute-start(f32[110,440]{1,0:T(8,128)S(1)} %collective-permute-done), channel_id=1, source_target_pairs={{0,1},{1,2},{2,3},{3,0},{4,5},{5,6},{6,7},{7,4},{8,9},{9,10},{10,1... | collective-permute-start | bytes 580808 | tf_op jit(solution)/shard_map/ppermute | solution.py:19
  310.1 8.0 %collective-permute-start.2 = (f32[110,440]{1,0:T(8,128)S(1)}, f32[110,440]{1,0:T(8,128)S(1)}, u32[]{:S(2)}, u32[]{:S(2)}) collective-permute-start(f32[110,440]{1,0:T(8,128)S(1)} %collective-permute-done.1), channel_id=1, source_target_pairs={{0,1},{1,2},{2,3},{3,0},{4,5},{5,6},{6,7},{7,4},{8,9},{9,10},{10,1... | collective-permute-start | bytes 580808 | tf_op jit(solution)/shard_map/ppermute | solution.py:19
Sparse Core Ops, SparseCore 0:
  40.5 73.7 all-gather.2
  116.2 32.6 all-gather.4
  216.4 74.7 all-reduce.3
